TPU v7x, 32 devices: a whole 2x2x4 slice. The times are simulated.
32 devices in a mesh: dp: 4 (over y, x), seq: 8 (over z, core).
Axes of the slice: x: 2, y: 2, z: 4, core: 2. Of those that a mesh axis runs over, the one named last changes fastest.
Arguments:
- block_input: bfloat16 [4, 1024, 1024], P('dp', 'seq'), may hold values from -6 to 6
- in_w: bfloat16 [1024, 3072], P(('dp', 'seq')), may hold values from -0.1875 to 0.1875
- out_w: bfloat16 [1024, 1024], P(('dp', 'seq')), may hold values from -0.1875 to 0.1875
- w_gate: bfloat16 [1024, 4608], P(('dp', 'seq')), may hold values from -0.1875 to 0.1875
- w_up: bfloat16 [1024, 4608], P(('dp', 'seq')), may hold values from -0.1875 to 0.1875
- w_down: bfloat16 [4608, 1024], P(('dp', 'seq')), may hold values from -0.125 to 0.125
- gain_mix: bfloat16 [1024], P(('dp', 'seq')), may hold values from 0.099609375 to 1.8984375
- gain_ffn: bfloat16 [1024], P(('dp', 'seq')), may hold values from 0.099609375 to 1.8984375
- conv_taps: bfloat16 [3, 1024], P(None, ('dp', 'seq')), may hold values from -3 to 3
- output_grad: bfloat16 [4, 1024, 1024], P('dp', 'seq'), may hold values from -6 to 6
Outputs:
- block_output: bfloat16 [4, 1024, 1024], P('dp', 'seq')
- input_grad: float32 [4, 1024, 1024], P('dp', 'seq')
- d_in_w: float32 [1024, 3072], P(('dp', 'seq'))
- d_out_w: float32 [1024, 1024], P(('dp', 'seq'))
- d_w_gate: float32 [1024, 4608], P(('dp', 'seq'))
- d_w_up: float32 [1024, 4608], P(('dp', 'seq'))
- d_w_down: float32 [4608, 1024], P(('dp', 'seq'))
- d_gain_mix: float32 [1024], P(('dp', 'seq'))
- d_gain_ffn: float32 [1024], P(('dp', 'seq'))
- d_conv_taps: float32 [3, 1024], P(None, ('dp', 'seq'))
All inputs are finite; a program needn't handle non-finite values.
Results may differ from a plain program's by a relative error of at most 0.011.
Values may be sent and summed in bfloat16 or wider, within the bound.
No kernel may reach another device: no remote copies, remote signals or barrier semaphores. Data moves between devices by JAX's collectives and lax.ppermute only.
A program may use at most 192 MiB of HBM per device.

v0:
```python
import jax
import jax.numpy as jnp
from jax import lax
from jax.sharding import PartitionSpec as P

EPS = 1e-05


def shifted(value, axis, steps):
    count = lax.axis_size(axis)
    leading, last = (max(0, -steps), min(count, count - steps))
    return lax.ppermute(value, axis, [(source, source + steps) for source in range(leading, last)])


def norm_fwd(values, gain):
    scale = lax.rsqrt(jnp.mean(values * values, -1, keepdims=True) + EPS)
    return (values * scale * gain, scale)


def norm_bwd(values, scale, gain, grad):
    hat = values * scale
    inner = grad * gain
    dvalues = scale * (inner - hat * jnp.mean(inner * hat, -1, keepdims=True))
    return (dvalues, jnp.sum(grad * hat, 0))


def tdot(left, right):
    return lax.dot_general(
        left, right, (((0,), (0,)), ((), ())), preferred_element_type=jnp.float32
    )


def bdot(left, right):
    return lax.dot_general(
        left, right, (((1,), (1,)), ((), ())), preferred_element_type=jnp.float32
    )


def shards(
    block_input, in_w, out_w, w_gate, w_up, w_down, gain_mix, gain_ffn, conv_taps, output_grad
):
    seqs_here = block_input.shape[0]
    group = block_input.shape[1]
    width = block_input.shape[2]
    rows = seqs_here * group
    full = (
        lax.all_gather(in_w, ("dp", "seq"), axis=0, tiled=True),
        lax.all_gather(out_w, ("dp", "seq"), axis=0, tiled=True),
        lax.all_gather(w_gate, ("dp", "seq"), axis=0, tiled=True),
        lax.all_gather(w_up, ("dp", "seq"), axis=0, tiled=True),
        lax.all_gather(w_down, ("dp", "seq"), axis=0, tiled=True),
        lax.all_gather(gain_mix, ("dp", "seq"), axis=0, tiled=True),
        lax.all_gather(gain_ffn, ("dp", "seq"), axis=0, tiled=True),
        lax.all_gather(conv_taps, ("dp", "seq"), axis=1, tiled=True),
    )
    f_in, f_out, f_gate, f_up, f_down, f_gmix, f_gffn, f_taps = full
    xf = block_input.reshape(rows, width).astype(jnp.float32)
    gmix = f_gmix.astype(jnp.float32)
    gffn = f_gffn.astype(jnp.float32)
    tapf = f_taps.astype(jnp.float32)
    h1, s1 = norm_fwd(xf, gmix)
    a1 = h1.astype(jnp.bfloat16)
    proj = jnp.dot(a1, f_in, preferred_element_type=jnp.float32)
    bgate = proj[:, :width]
    cgate = proj[:, width : 2 * width]
    value = proj[:, 2 * width :]
    bx = (bgate * value).astype(jnp.bfloat16).reshape(seqs_here, group, width)
    edge = shifted(bx[:, group - 2 :, :], "seq", 1)
    ext = jnp.concatenate([edge, bx], 1).astype(jnp.float32)
    conv = tapf[0] * ext[:, :group] + tapf[1] * ext[:, 1 : group + 1] + tapf[2] * ext[:, 2:]
    conv = conv.reshape(rows, width)
    a2 = (cgate * conv).astype(jnp.bfloat16)
    resid = xf + jnp.dot(a2, f_out, preferred_element_type=jnp.float32)
    h2, s2 = norm_fwd(resid, gffn)
    a3 = h2.astype(jnp.bfloat16)
    gates = jnp.dot(a3, f_gate, preferred_element_type=jnp.float32)
    upper = jnp.dot(a3, f_up, preferred_element_type=jnp.float32)
    sigm = jax.nn.sigmoid(gates)
    active = gates * sigm
    hid = (active * upper).astype(jnp.bfloat16)
    result = (resid + jnp.dot(hid, f_down, preferred_element_type=jnp.float32)).astype(jnp.bfloat16)
    again = (
        lax.all_gather(in_w, ("dp", "seq"), axis=0, tiled=True),
        lax.all_gather(out_w, ("dp", "seq"), axis=0, tiled=True),
        lax.all_gather(w_gate, ("dp", "seq"), axis=0, tiled=True),
        lax.all_gather(w_up, ("dp", "seq"), axis=0, tiled=True),
        lax.all_gather(w_down, ("dp", "seq"), axis=0, tiled=True),
        lax.all_gather(gain_mix, ("dp", "seq"), axis=0, tiled=True),
        lax.all_gather(gain_ffn, ("dp", "seq"), axis=0, tiled=True),
        lax.all_gather(conv_taps, ("dp", "seq"), axis=1, tiled=True),
    )
    b_in, b_out, b_gate, b_up, b_down, b_gmix, b_gffn, b_taps = again
    gmix = b_gmix.astype(jnp.float32)
    gffn = b_gffn.astype(jnp.float32)
    tapf = b_taps.astype(jnp.float32)
    dys = output_grad.reshape(rows, width)
    dyf = dys.astype(jnp.float32)
    d_down = tdot(hid, dys)
    dhid = bdot(dys, b_down)
    dgate = (dhid * upper * (sigm * (1.0 + gates * (1.0 - sigm)))).astype(jnp.bfloat16)
    dupper = (dhid * active).astype(jnp.bfloat16)
    d_gate = tdot(a3, dgate)
    d_up = tdot(a3, dupper)
    da3 = bdot(dgate, b_gate) + bdot(dupper, b_up)
    dres, dg_ffn = norm_bwd(resid, s2, gffn, da3)
    dres = dres + dyf
    drb = dres.astype(jnp.bfloat16)
    d_out = tdot(a2, drb)
    da2 = bdot(drb, b_out)
    dcgate = da2 * conv
    dconv = (da2 * cgate).reshape(seqs_here, group, width)
    after = shifted(dconv[:, :2, :], "seq", -1)
    extd = jnp.concatenate([dconv, after], 1)
    dbx = tapf[2] * extd[:, :group] + tapf[1] * extd[:, 1 : group + 1] + tapf[0] * extd[:, 2:]
    dtaps = jnp.stack([jnp.sum(dconv * ext[:, k : k + group], (0, 1)) for k in range(3)], 0)
    dbx = dbx.reshape(rows, width)
    dproj = jnp.concatenate([dbx * value, dcgate, dbx * bgate], 1).astype(jnp.bfloat16)
    d_in = tdot(a1, dproj)
    da1 = bdot(dproj, b_in)
    dx1, dg_mix = norm_bwd(xf, s1, gmix, da1)
    dxs = (dres + dx1).reshape(seqs_here, group, width)
    summed = (
        lax.psum_scatter(d_in, ("dp", "seq"), scatter_dimension=0, tiled=True),
        lax.psum_scatter(d_out, ("dp", "seq"), scatter_dimension=0, tiled=True),
        lax.psum_scatter(d_gate, ("dp", "seq"), scatter_dimension=0, tiled=True),
        lax.psum_scatter(d_up, ("dp", "seq"), scatter_dimension=0, tiled=True),
        lax.psum_scatter(d_down, ("dp", "seq"), scatter_dimension=0, tiled=True),
        lax.psum_scatter(dg_mix, ("dp", "seq"), scatter_dimension=0, tiled=True),
        lax.psum_scatter(dg_ffn, ("dp", "seq"), scatter_dimension=0, tiled=True),
        lax.psum_scatter(dtaps, ("dp", "seq"), scatter_dimension=1, tiled=True),
    )
    return (
        result.reshape(seqs_here, group, width),
        dxs,
        summed[0],
        summed[1],
        summed[2],
        summed[3],
        summed[4],
        summed[5],
        summed[6],
        summed[7],
    )


def solution(mesh):
    return jax.shard_map(
        shards,
        mesh=mesh,
        in_specs=(
            P("dp", "seq", None),
            P(("dp", "seq"), None),
            P(("dp", "seq"), None),
            P(("dp", "seq"), None),
            P(("dp", "seq"), None),
            P(("dp", "seq"), None),
            P(("dp", "seq")),
            P(("dp", "seq")),
            P(None, ("dp", "seq")),
            P("dp", "seq", None),
        ),
        out_specs=(
            P("dp", "seq", None),
            P("dp", "seq", None),
            P(("dp", "seq"), None),
            P(("dp", "seq"), None),
            P(("dp", "seq"), None),
            P(("dp", "seq"), None),
            P(("dp", "seq"), None),
            P(("dp", "seq")),
            P(("dp", "seq")),
            P(None, ("dp", "seq")),
        ),
        check_vma=False,
    )
```

profile of v0, /device:TPU:0, one launch (start us, length us, event | category | flops | bytes accessed | tf_op | source)
XLA Modules:
  0.0 1496.3 jit_solution(16850573063885946554)
XLA Ops:
  12.3 42.4 %all-reduce.5 = (bf16[1024]{0:T(1024)(128)(2,1)S(1)}, bf16[1024]{0:T(1024)(128)(2,1)S(1)}) all-reduce(bf16[1024]{0:T(1024)(128)(2,1)S(1)} %dynamic-update-slice, bf16[1024]{0:T(1024)(128)(2,1)S(1)} %dynamic-update-slice.1), channel_id=1, replica_groups=mesh['dp'=4,'seq'=8] {'dp','seq'}, use_global_device_ids=true, to_apply=%add | all-reduce | flops 2048 | bytes 8192
  54.7 41.2 %all-gather = bf16[32,32,3]{1,2,0:T(4,128)(2,1)S(1)} all-gather(bf16[1,32,3]{1,2,0:T(4,128)(2,1)} %bitcast.90), channel_id=1, replica_groups=mesh['dp'=4,'seq'=8] {'dp','seq'}, dimensions={0}, use_global_device_ids=true | all-gather | bytes 6336 | tf_op jit(solution)/shard_map/all_gather | solution.py:54
  97.2 4.0 fusion.36
  101.2 2.4 collective-permute-start
  105.4 36.1 %all-gather.9.cloned.1.call-done = bf16[1024,1024]{1,0:T(8,128)(2,1)} async-done(((bf16[32,1024]{1,0:T(8,128)(2,1)}), bf16[1024,1024]{1,0:T(8,128)(2,1)}) %all-gather.9.cloned.1.call-update) | async-done | bytes 2097168 | tf_op jit(solution)/shard_map/all_gather | solution.py:48
  141.4 2.1 multiply_reduce_fusion.5
  143.7 81.2 %all-gather.11.cloned.1.call-done = bf16[1024,4608]{1,0:T(8,128)(2,1)} async-done(((bf16[32,4608]{1,0:T(8,128)(2,1)}), bf16[1024,4608]{1,0:T(8,128)(2,1)}) %all-gather.11.cloned.1.call-update) | async-done | bytes 9437200 | tf_op jit(solution)/shard_map/all_gather | solution.py:49
  224.9 6.5 fusion.43
  231.4 76.5 %all-gather.13.cloned.1.call-done = bf16[1024,4608]{1,0:T(8,128)(2,1)} async-done(((bf16[32,4608]{1,0:T(8,128)(2,1)}), bf16[1024,4608]{1,0:T(8,128)(2,1)}) %all-gather.13.cloned.1.call-update) | async-done | bytes 9437200 | tf_op jit(solution)/shard_map/all_gather | solution.py:50
  307.9 6.5 fusion.44
  314.4 76.4 %all-gather.15.cloned.1.call-done = bf16[4608,1024]{1,0:T(8,128)(2,1)} async-done(((bf16[144,1024]{1,0:T(8,128)(2,1)}), bf16[4608,1024]{1,0:T(8,128)(2,1)}) %all-gather.15.cloned.1.call-update) | async-done | bytes 9437200 | tf_op jit(solution)/shard_map/all_gather | solution.py:51
  390.8 9.7 multiply_convert_fusion
  400.6 7.7 fusion.45
  408.3 3.2 multiply_reduce_fusion.3
  414.7 3.8 fusion.31
  419.4 1.5 collective-permute-start.1
  420.9 1.5 collective-permute-done.1
  422.4 1.8 multiply_convert_fusion.4
  425.0 6.4 fusion.23
  432.7 8.0 fusion.46
  441.9 7.9 fusion.47
  451.1 7.8 fusion.26
  458.9 6.3 fusion.2
  465.3 3.0 fusion.18
  468.3 40.7 %all-reduce.4 = (f32[1024]{0:T(1024)S(1)}, f32[1024]{0:T(1024)S(1)}) all-reduce(f32[1024]{0:T(1024)S(1)} %get-tuple-element.15, f32[1024]{0:T(1024)S(1)} %get-tuple-element.13), channel_id=7, replica_groups=mesh['dp'=4,'seq'=8] {'dp','seq'}, use_global_device_ids=true, to_apply=%region_10.0.clone | all-reduce | flops 2048 | bytes 16384
  510.2 2.1 fusion.17
  512.3 37.0 %reduce-scatter.19.cloned.1.call-done = f32[32,3]{1,0:T(8,128)} async-done(((f32[1024,3]{1,0:T(8,128)}), f32[32,3]{1,0:T(8,128)}) %reduce-scatter.19.cloned.1.call-update) | async-done | bytes 400
  550.6 141.6 %reduce-scatter.11.cloned.1.call-done = f32[32,1024]{1,0:T(8,128)} async-done(((f32[1024,1024]{1,0:T(8,128)}), f32[32,1024]{1,0:T(8,128)}) %reduce-scatter.11.cloned.1.call-update) | async-done | bytes 131088 | tf_op jit(solution)/shard_map/reduce_scatter | solution.py:124
  692.2 158.6 %reduce-scatter.9.cloned.1.call-done = f32[32,3072]{1,0:T(8,128)} async-done(((f32[1024,3072]{1,0:T(8,128)}), f32[32,3072]{1,0:T(8,128)}) %reduce-scatter.9.cloned.1.call-update) | async-done | bytes 393232 | tf_op jit(solution)/shard_map/reduce_scatter | solution.py:123
  850.8 212.8 %reduce-scatter.13.cloned.1.call-done = f32[32,4608]{1,0:T(8,128)} async-done(((f32[1024,4608]{1,0:T(8,128)}), f32[32,4608]{1,0:T(8,128)}) %reduce-scatter.13.cloned.1.call-update) | async-done | bytes 589840 | tf_op jit(solution)/shard_map/reduce_scatter | solution.py:125
  1063.7 213.0 %reduce-scatter.15.cloned.1.call-done = f32[32,4608]{1,0:T(8,128)} async-done(((f32[1024,4608]{1,0:T(8,128)}), f32[32,4608]{1,0:T(8,128)}) %reduce-scatter.15.cloned.1.call-update) | async-done | bytes 589840 | tf_op jit(solution)/shard_map/reduce_scatter | solution.py:126
  1276.6 213.2 %reduce-scatter.17.cloned.1.call-done = f32[144,1024]{1,0:T(8,128)} async-done(((f32[4608,1024]{1,0:T(8,128)}), f32[144,1024]{1,0:T(8,128)}) %reduce-scatter.17.cloned.1.call-update) | async-done | bytes 589840 | tf_op jit(solution)/shard_map/reduce_scatter | solution.py:127
  (94 shorter events, 19.3 us)
Async XLA Ops:
  7.2 90.0 %all-gather.7.cloned.1.call-start = ((), (), s32[]{:S(2)}) async-start(), calls=%async_computation.6 | async-start | bytes 6488064 | tf_op jit(solution)/shard_map/all_gather | solution.py:47
  7.9 133.5 %all-gather.9.cloned.1.call-start = ((), (), s32[]{:S(2)}) async-start(), calls=%async_computation.7 | async-start | bytes 2162688 | tf_op jit(solution)/shard_map/all_gather | solution.py:48
  8.7 216.2 %all-gather.11.cloned.1.call-start = ((), (), s32[]{:S(2)}) async-start(), calls=%async_computation.8 | async-start | bytes 9732096 | tf_op jit(solution)/shard_map/all_gather | solution.py:49
  9.4 298.5 %all-gather.13.cloned.1.call-start = ((), (), s32[]{:S(2)}) async-start(), calls=%async_computation.9 | async-start | bytes 9732096 | tf_op jit(solution)/shard_map/all_gather | solution.py:50
  10.0 380.9 %all-gather.15.cloned.1.call-start = ((), (), s32[]{:S(2)}) async-start(), calls=%async_computation.10 | async-start | bytes 9732096 | tf_op jit(solution)/shard_map/all_gather | solution.py:51
  10.6 538.7 %reduce-scatter.19.cloned.1.call-start = ((), (), s32[]{:S(2)}) async-start(), calls=%async_computation.16 | async-start | bytes 540672
  101.1 40.3 %copy-start.2 = (bf16[1,128,1024]{2,1,0:T(8,128)(2,1)S(1)}, bf16[1,128,1024]{2,1,0:T(8,128)(2,1)}, u32[]{:S(2)}) copy-start(bf16[1,128,1024]{2,1,0:T(8,128)(2,1)} %param.10) | copy-start | bytes 786436
  101.2 3.1 collective-permute-start
  400.5 7.7 copy-start.8
  400.5 7.7 copy-start.6
  400.5 7.7 copy-start
  408.2 3.2 copy-start.12
  408.3 3.4 copy-start.5
  411.7 1.8 copy-start.3
  412.6 1.0 copy-start.10
  414.6 277.6 %reduce-scatter.11.cloned.1.call-start = ((), (), s32[]{:S(2)}) async-start(), calls=%async_computation.12 | async-start | bytes 4325376 | tf_op jit(solution)/shard_map/reduce_scatter | solution.py:124
  418.5 3.9 copy-start.11
  418.5 432.3 %reduce-scatter.9.cloned.1.call-start = ((), (), s32[]{:S(2)}) async-start(), calls=%async_computation.11 | async-start | bytes 12976128 | tf_op jit(solution)/shard_map/reduce_scatter | solution.py:123
  419.4 3.1 collective-permute-start.1
  424.2 0.7 copy-start.14
  431.4 1.3 copy-start.9
  431.4 632.2 %reduce-scatter.13.cloned.1.call-start = ((), (), s32[]{:S(2)}) async-start(), calls=%async_computation.13 | async-start | bytes 19464192 | tf_op jit(solution)/shard_map/reduce_scatter | solution.py:125
  440.6 1.3 copy-start.7
  440.7 836.0 %reduce-scatter.15.cloned.1.call-start = ((), (), s32[]{:S(2)}) async-start(), calls=%async_computation.14 | async-start | bytes 19464192 | tf_op jit(solution)/shard_map/reduce_scatter | solution.py:126
  449.8 1.3 copy-start.1
  449.8 1.3 copy-start.13
  449.8 1040.0 %reduce-scatter.17.cloned.1.call-start = ((), (), s32[]{:S(2)}) async-start(), calls=%async_computation.15 | async-start | bytes 19464192 | tf_op jit(solution)/shard_map/reduce_scatter | solution.py:127
  458.9 6.4 slice-start
  458.9 6.4 slice-start.1
  458.9 6.3 copy-start.15
  458.9 6.3 copy-start.17
  465.3 44.9 %copy-start.4 = (f32[128,1024]{1,0:T(8,128)S(1)}, f32[128,1024]{1,0:T(8,128)}, u32[]{:S(2)}) copy-start(f32[128,1024]{1,0:T(8,128)} %copy-done.3) | copy-start | bytes 1572868
  (1 other events, 0.7 us)
Sparse Core Ops, SparseCore 0:
  11.0 72.3 all-gather.6
  86.4 54.9 all-gather.8
  144.4 80.3 all-gather.10
  227.8 80.0 all-gather.12
  310.7 80.0 all-gather.14
  414.8 134.4 reduce-scatter.18
  552.1 140.0 reduce-scatter.10
  698.8 152.0 reduce-scatter.8
  857.8 205.7 reduce-scatter.12
  1070.5 206.0 reduce-scatter.14
  1283.6 206.1 reduce-scatter.16
where the time goes:
time: 1500 us
  waiting for transfers between devices  1250 us (83%)
  blocking collectives  124 us (8%)
  matrix products  83.6 us (6%)
    reduce_scatter x1, waiting for transfers between devices, shards(): lax.psum_scatter(d_down, ('dp', 'seq'), scatter_dimension=0, tiled=True)  213 us
    reduce_scatter x1, waiting for transfers between devices, shards(): lax.psum_scatter(d_up, ('dp', 'seq'), scatter_dimension=0, tiled=True)  213 us
    reduce_scatter x1, waiting for transfers between devices, shards(): lax.psum_scatter(d_gate, ('dp', 'seq'), scatter_dimension=0, tiled=True)  213 us
    reduce_scatter x1, waiting for transfers between devices, shards(): lax.psum_scatter(d_in, ('dp', 'seq'), scatter_dimension=0, tiled=True)  159 us
    reduce_scatter x1, waiting for transfers between devices, shards(): lax.psum_scatter(d_out, ('dp', 'seq'), scatter_dimension=0, tiled=True)  142 us
    unnamed x2, blocking collectives  83.1 us
    all_gather x1, waiting for transfers between devices, shards(): lax.all_gather(w_gate, ('dp', 'seq'), axis=0, tiled=True)  81.2 us
    all_gather x1, waiting for transfers between devices, shards(): lax.all_gather(w_up, ('dp', 'seq'), axis=0, tiled=True)  76.5 us
  transfers between devices with their start and end apart: 13, of which 12 were waited for; matrix products, arithmetic and copies ran while one was open for 5% of the time, Pallas kernels for 0%

commit v1 on v0

v1 whole, which is shorter than its diff:
```python
import functools

import jax
import jax.numpy as jnp
from jax import lax
from jax.experimental import pallas as pl
from jax.experimental.pallas import tpu as pltpu
from jax.sharding import PartitionSpec as P


EPS = 1e-05
BF = jnp.bfloat16
F32 = jnp.float32
SMEM = pl.BlockSpec(memory_space=pltpu.SMEM)
VMEM = pl.BlockSpec(memory_space=pltpu.VMEM)


def dot(left, right):
    return jnp.dot(left, right, preferred_element_type=F32)


def tdot(left, right):
    return lax.dot_general(left, right, (((0,), (0,)), ((), ())), preferred_element_type=F32)


def bdot(left, right):
    return lax.dot_general(left, right, (((1,), (1,)), ((), ())), preferred_element_type=F32)


def normed(values):
    scale = lax.rsqrt(jnp.mean(values * values, -1, keepdims=True) + EPS)
    return values * scale, scale


def norm_bwd(hat, scale, inner):
    return scale * (inner - hat * jnp.mean(inner * hat, -1, keepdims=True))


def after(value, *earlier):
    return lax.optimization_barrier((value,) + earlier)[0]


def chips():
    return lax.axis_size("seq") // 2


def to_chip(block, k):
    return lax.ppermute(block, "seq", [(i, i ^ (2 * k)) for i in range(lax.axis_size("seq"))])


def swap(block):
    return lax.ppermute(block, "seq", [(i, i ^ 1) for i in range(lax.axis_size("seq"))])


def to_row(block, k):
    return lax.ppermute(block, "dp", [(i, i ^ k) for i in range(lax.axis_size("dp"))])


def gather_seq(block, hold=()):
    blocks = [block] + [to_chip(block, k) for k in range(1, chips())]
    blocks = list(after(tuple(blocks), *hold))
    return [b for mine in blocks for b in (mine, swap(mine))]


def gather_dp(block):
    return [block] + [to_row(block, k) for k in range(1, lax.axis_size("dp"))]


def meet(near, far, rows):
    got = swap(far)
    if not isinstance(near, (list, tuple)):
        near = [near[k : k + rows] for k in range(0, near.shape[0], rows)]
    return [n + got[k * rows : (k + 1) * rows].astype(F32) for k, n in enumerate(near)]


def send_seq(met):
    sent = [m.astype(BF) for m in met[1:]]
    total = met[0]
    for k, part in enumerate(sent):
        total = total + to_chip(part, k + 1).astype(F32)
    return total, sent


def send_dp(pieces, hold=()):
    got = tuple(to_row(part, k + 1) for k, part in enumerate(pieces[1:]))
    total = pieces[0]
    for part in after(got, *hold):
        total = total + part.astype(F32)
    return total


def columns_of(weight, parts):
    dp, seq = lax.axis_size("dp"), lax.axis_size("seq")
    rows, columns = weight.shape
    unit = columns // (parts * dp * seq)
    cut = weight.reshape(rows, parts * dp, seq, unit).transpose(2, 0, 1, 3)
    return cut.reshape(seq, rows, parts * dp * unit)


def exchange(pieces):
    return lax.all_to_all(pieces, "seq", 0, 0, tiled=True)


def rows_of(pieces, parts):
    seq, rows, columns = pieces.shape
    unit = columns // (parts * lax.axis_size("dp"))
    back = pieces.reshape(seq, rows, columns // unit, unit).transpose(1, 2, 0, 3)
    return back.reshape(rows, columns * seq).astype(F32)


def call(kernel, out, smem, inputs, scratch=()):
    out_shape = [jax.ShapeDtypeStruct(shape, dtype) for shape, dtype in out]
    return pl.pallas_call(
        kernel,
        out_shape=out_shape,
        in_specs=[SMEM] * len(smem) + [VMEM] * len(inputs),
        out_specs=[VMEM] * len(out),
        scratch_shapes=list(scratch),
    )(*smem, *inputs)


def at(index, rows):
    return pl.ds(pl.multiple_of(index * rows, rows), rows)


def chosen(index, values):
    total = jnp.zeros_like(values[0])
    for i, value in enumerate(values):
        total = jnp.where(index == i, value, total)
    return total


def place(blocks, whole, where):
    rows = blocks[0].shape[0]
    if rows % 8 == 0:
        for j, block in enumerate(blocks):
            whole[at(where[j], rows), :] = block[...]
        return
    for j, block in enumerate(blocks):
        for i in range(len(blocks)):

            @pl.when(where[j] == i)
            def _():
                whole[i * rows : (i + 1) * rows, :] = block[...]


def take(whole, pieces, where):
    rows = pieces[0].shape[0]
    for k, ref in enumerate(pieces):
        if rows % 8 == 0:
            value = whole[at(where[k], rows), :]
        else:
            values = [whole[i * rows : (i + 1) * rows, :] for i in range(len(pieces))]
            value = chosen(where[k], values)
        ref[...] = value.astype(ref.dtype)


def shift_rows(values, steps):
    rows = values.shape[0]
    row = lax.broadcasted_iota(jnp.int32, values.shape, 0)
    kept = row >= steps if steps > 0 else row < rows + steps
    return jnp.where(kept, pltpu.roll(values, steps % rows, 0), 0.0)


def split(refs, *counts):
    start = 0
    for count in counts:
        yield refs[start : start + count]
        start += count


def mixer_parts(proj, taps, chans):
    bgate, cgate, value = proj[:, :chans], proj[:, chans : 2 * chans], proj[:, 2 * chans :]
    bx = (bgate * value).astype(BF).astype(F32)
    bx1, bx2 = shift_rows(bx, 1), shift_rows(bx, 2)
    conv = taps[0:1] * bx2 + taps[1:2] * bx1 + taps[2:3] * bx
    return bgate, cgate, value, bx, bx1, bx2, conv


def put_slots(part, near, far, where, rows):
    for k, ref in enumerate(near):
        ref[...] = part[at(where[2 * k], rows), :]
        far[k * rows : (k + 1) * rows, :] = part[at(where[2 * k + 1], rows), :].astype(BF)


def mixer_kernel(slots, dps, where, dwhere, *refs):
    xs, ins, outs, res = split(refs, slots, dps, dps, 7 + slots // 2 + 2)
    a1, win, wout, proj_ref, a2_ref, gains, taps = res[:7]
    near, far, part = res[7:-2], res[-2], res[-1]
    rows, width = xs[0].shape
    chans = wout.shape[0]
    place(ins, win, dwhere)
    place(outs, wout, dwhere)
    gain = jnp.transpose(win[:, 3 * chans :].astype(F32))[: gains.shape[0]]
    gains[...] = gain
    tap = jnp.transpose(wout[:, width:].astype(F32))[: taps.shape[0]]
    taps[...] = tap
    for j, x in enumerate(xs):
        hat = normed(x[...].astype(F32))[0]
        a1[at(where[j], rows), :] = (hat * gain[0:1]).astype(BF)
    proj = dot(a1[...], win[:, : 3 * chans])
    proj_ref[...] = proj
    _, cgate, _, _, _, _, conv = mixer_parts(proj, tap, chans)
    a2 = (cgate * conv).astype(BF)
    a2_ref[...] = a2
    part[...] = dot(a2, wout[:, :width])
    put_slots(part, near, far, where, rows)


def mixer(where, dwhere, xs, ins, outs):
    rows, width = xs[0].shape
    length = rows * len(xs)
    chans = outs[0].shape[0] * len(outs)
    out = [
        ((length, width), BF),
        ((width, ins[0].shape[1]), BF),
        ((chans, outs[0].shape[1]), BF),
        ((length, 3 * chans), F32),
        ((length, chans), BF),
        ((8, width), F32),
        ((8, chans), F32),
    ]
    out += [((rows, width), F32)] * (len(xs) // 2) + [((length // 2, width), BF)]
    kernel = functools.partial(mixer_kernel, len(xs), len(ins))
    res = call(kernel, out, [where, dwhere], [*xs, *ins, *outs], [pltpu.VMEM((length, width), F32)])
    return res[:5], res[5], res[6], res[7:-1], res[-1]


def mixer_bwd_kernel(slots, where, taps, win, wout, proj_ref, *refs):
    gs, res = split(refs, slots, slots // 2 + 5)
    near, far = res[: slots // 2], res[slots // 2]
    drb, dproj_ref, lines_ref, part = res[1 + slots // 2 :]
    rows, width = gs[0].shape
    chans = wout.shape[0]
    place(gs, drb, where)
    tap = taps[...]
    bgate, cgate, value, bx, bx1, bx2, conv = mixer_parts(proj_ref[...], tap, chans)
    da2 = bdot(drb[...], wout[:, :width])
    dconv = da2 * cgate
    dbx = tap[2:3] * dconv + tap[1:2] * shift_rows(dconv, -1) + tap[0:1] * shift_rows(dconv, -2)
    dproj = jnp.concatenate([dbx * value, da2 * conv, dbx * bgate], -1).astype(BF)
    dproj_ref[...] = dproj
    part[...] = bdot(dproj, win[:, : 3 * chans])
    put_slots(part, near, far, where, rows)
    lines_ref[...] = jnp.zeros_like(lines_ref)
    for k, v in enumerate((bx2, bx1, bx)):
        lines_ref[k : k + 1, :] = jnp.sum(dconv * v, 0, keepdims=True)


def mixer_grads_kernel(dps, dwhere, a1, a2, drb, dproj, lines, *refs):
    d_outs, d_ins, (d_out, d_in) = split(refs, dps, dps, 2)
    width = drb.shape[1]
    d_in[...] = tdot(a1[...], dproj[...])
    take(d_in, d_ins, dwhere)
    d_out[:, :width] = tdot(a2[...], drb[...])
    d_out[:, width:] = jnp.transpose(lines[...])
    take(d_out, d_outs, dwhere)


def pieces_of(shape, dps):
    return [(shape, F32)] + [(shape, BF)] * (dps - 1)


def mixer_bwd(where, taps, saved, gs):
    _, win, wout, proj, a2 = saved
    rows, width = gs[0].shape
    length, chans = a2.shape
    out = [((rows, width), F32)] * (len(gs) // 2) + [((length // 2, width), BF)]
    out += [((length, width), BF), ((length, 3 * chans), BF), ((128, chans), F32)]
    kernel = functools.partial(mixer_bwd_kernel, len(gs))
    scratch = [pltpu.VMEM((length, width), F32)]
    res = call(kernel, out, [where], [taps, win, wout, proj, *gs], scratch)
    return res[:-4], res[-4], res[-3:]


def mixer_grads(dwhere, saved, more):
    a1, _, wout, _, a2 = saved
    drb, dproj, lines = more
    dps = dwhere.shape[0]
    (width, chans), wide = (a1.shape[1], a2.shape[1]), wout.shape[1]
    out = pieces_of((chans // dps, wide), dps) + pieces_of((width // dps, 3 * chans), dps)
    scratch = [pltpu.VMEM((chans, wide), F32), pltpu.VMEM((width, 3 * chans), F32)]
    kernel = functools.partial(mixer_grads_kernel, dps)
    res = call(kernel, out, [dwhere], [a1, a2, drb, dproj, lines], scratch)
    return res[:dps], res[dps:]


def ffn_kernel(slots, dps, dwhere, *refs):
    xs, gs, wgus, wds, res = split(refs, slots, slots, dps, dps, 10)
    fed_near, fed_far, dn_near, dn_far, hid_ref, dgu_ref, wgu, wd, a3s, dys = res
    rows = xs[0].shape[0]
    units = wd.shape[0]
    place(wgus, wgu, dwhere)
    place(wds, wd, dwhere)
    for j in range(slots):
        a3s[j * rows : (j + 1) * rows, :] = xs[j][...]
        dys[j * rows : (j + 1) * rows, :] = gs[j][...]

    def step(k, _):
        two, one = at(k, 2 * rows), at(k, rows)
        both = dot(a3s[two, :], wgu[...])
        gates, upper = both[:, :units], both[:, units:]
        dhid = bdot(dys[two, :], wd[...])
        sigm = jax.nn.sigmoid(gates)
        active = gates * sigm
        hid = (active * upper).astype(BF)
        dgate = (dhid * upper * (sigm * (1.0 + gates * (1.0 - sigm)))).astype(BF)
        dgu = jnp.concatenate([dgate, (dhid * active).astype(BF)], 1)
        hid_ref[two, :] = hid
        dgu_ref[two, :] = dgu
        dn = bdot(dgu, wgu[...])
        dn_near[one, :] = dn[:rows]
        dn_far[one, :] = dn[rows:].astype(BF)
        fed = dot(hid, wd[...])
        fed_near[one, :] = fed[:rows]
        fed_far[one, :] = fed[rows:].astype(BF)
        return 0

    lax.fori_loop(0, slots // 2, step, 0)


def ffn(dwhere, xs, gs, wgus, wds):
    rows, width = xs[0].shape
    half, dps = len(xs) // 2, len(wds)
    units = wds[0].shape[0] * dps
    parts = [((half * rows, width), F32), ((half * rows, width), BF)]
    out = parts + parts + [((2 * half * rows, units), BF), ((2 * half * rows, 2 * units), BF)]
    scratch = [pltpu.VMEM((width, 2 * units), BF), pltpu.VMEM((units, width), BF)]
    scratch += [pltpu.VMEM((2 * half * rows, width), BF)] * 2
    kernel = functools.partial(ffn_kernel, len(xs), dps)
    res = call(kernel, out, [dwhere], [*xs, *gs, *wgus, *wds], scratch)
    return res[:2], res[2:4], res[4:]


def grads_kernel(slots, calls, dps, dwhere, *refs):
    xs, gs, hids, dgus, d_pairs, d_downs, res = split(
        refs, slots, slots, calls, calls, dps, dps, 6
    )
    a3, dys, hid, dgu, d_pair, d_down = res
    for blocks, whole in ((xs, a3), (gs, dys), (hids, hid), (dgus, dgu)):
        start = 0
        for block in blocks:
            whole[start : start + block.shape[0], :] = block[...]
            start += block.shape[0]
    d_pair[...] = tdot(a3[...], dgu[...])
    take(d_pair, d_pairs, dwhere)
    d_down[...] = tdot(hid[...], dys[...])
    take(d_down, d_downs, dwhere)


def grads(dwhere, xs, gs, mids):
    rows, width = xs[0].shape
    length = rows * len(xs)
    units = mids[0][0].shape[1]
    dps = dwhere.shape[0]
    out = pieces_of((width // dps, 2 * units), dps) + pieces_of((units // dps, width), dps)
    scratch = [pltpu.VMEM((length, width), BF)] * 2
    scratch += [pltpu.VMEM((length, units), BF), pltpu.VMEM((length, 2 * units), BF)]
    scratch += [pltpu.VMEM((width, 2 * units), F32), pltpu.VMEM((units, width), F32)]
    kernel = functools.partial(grads_kernel, len(xs), len(mids), dps)
    flat = [m[0] for m in mids] + [m[1] for m in mids]
    res = call(kernel, out, [dwhere], [*xs, *gs, *flat], scratch)
    return res[:dps], res[dps:]


def fill(values, columns):
    return jnp.pad(values, ((0, 0), (0, columns - values.shape[1])))


def shards(
    block_input, in_w, out_w, w_gate, w_up, w_down, gain_mix, gain_ffn, conv_taps, output_grad
):
    seqs, group, width = block_input.shape
    rows = seqs * group
    assert seqs == 1
    chip, core, row = lax.axis_index("seq") // 2, lax.axis_index("seq") % 2, lax.axis_index("dp")
    slot = jnp.arange(lax.axis_size("seq"), dtype=jnp.int32)
    where = 2 * (chip ^ (slot // 2)) + (core ^ (slot % 2))
    dwhere = row ^ jnp.arange(lax.axis_size("dp"), dtype=jnp.int32)

    seq, lanes = lax.axis_size("seq"), 128
    x_rows, g_rows = block_input.reshape(rows, width), output_grad.reshape(rows, width)
    pair = columns_of(jnp.concatenate([w_gate, w_up], 1), 2)
    xs = gather_seq(x_rows, (pair,))
    unit = in_w.shape[0]
    gains = fill(jnp.stack([gain_mix, gain_ffn], 1), lanes)
    cols = jnp.concatenate(
        [columns_of(in_w, 3), jnp.broadcast_to(gains, (seq,) + gains.shape)], 2
    )
    cols = exchange(cols).reshape(seq * unit, -1)
    ins = gather_dp(cols)
    outs = gather_dp(jnp.concatenate([out_w, fill(conv_taps.transpose(1, 0), lanes)], 1))
    wds = gather_dp(w_down)
    pair = exchange(pair)
    wgus = gather_dp(pair.reshape(seq * unit, -1))
    gs = gather_seq(g_rows)

    xf = x_rows.astype(F32)
    hat1, s1 = normed(xf)
    saved, gains, taps, near, far = mixer(where, dwhere, xs, ins, outs)
    gmix, gffn = gains[0:1], gains[1:2]
    resid = xf + send_seq(meet(near, far, rows))[0]
    hat2, s2 = normed(resid)

    a3s = gather_seq((hat2 * gffn).astype(BF))
    first = ffn(dwhere, a3s[:2], gs[:2], wgus, wds)
    later = ffn(dwhere, a3s[2:], gs[2:], wgus, wds)
    met = meet(*first[1], rows) + meet(*later[1], rows)
    da3, _ = send_seq(met)
    gf = g_rows.astype(F32)
    dres = gf + norm_bwd(hat2, s2, da3 * gffn)

    d_pairs, d_downs = grads(dwhere, a3s, gs, (first[2], later[2]))
    drbs = gather_seq(dres.astype(BF))
    met = meet(*first[0], rows) + meet(*later[0], rows)
    fed, _ = send_seq(met)
    result = (resid + fed).astype(BF)
    near, far, more = mixer_bwd(where, taps, saved, drbs)
    d_outs, d_ins = mixer_grads(dwhere, saved, more)
    da1, sent = send_seq(meet(near, far, rows))
    dxs = dres + norm_bwd(hat1, s1, da1 * gmix)

    e_in = send_dp(d_ins)
    d_in = rows_of(exchange(e_in.astype(BF).reshape(seq, unit, -1)), 3)
    d_out = send_dp(d_outs)
    d_out, dtaps = d_out[:, :width], d_out[:, width : width + 3].transpose(1, 0)

    d_down = send_dp(d_downs, sent)
    e_pair = send_dp(d_pairs, sent)
    e_pair = rows_of(exchange(e_pair.astype(BF).reshape(seq, unit, -1)), 2)
    d_gate, d_up = e_pair[:, : w_gate.shape[1]], e_pair[:, w_gate.shape[1] :]
    wsum = jnp.sum(d_gate * w_gate.astype(F32), 1) + jnp.sum(d_up * w_up.astype(F32), 1)
    dg_ffn = wsum / gain_ffn.astype(F32)
    dg_mix = jnp.sum(d_in * in_w.astype(F32), 1) / gain_mix.astype(F32)
    return (
        result.reshape(seqs, group, width),
        dxs.reshape(seqs, group, width),
        d_in,
        d_out,
        d_gate,
        d_up,
        d_down,
        dg_mix,
        dg_ffn,
        dtaps,
    )


def solution(mesh):
    flat = P(("dp", "seq"), None)
    acts = P("dp", "seq", None)
    vec = P(("dp", "seq"))
    taps = P(None, ("dp", "seq"))
    return jax.shard_map(
        shards,
        mesh=mesh,
        in_specs=(acts, flat, flat, flat, flat, flat, vec, vec, taps, acts),
        out_specs=(acts, acts, flat, flat, flat, flat, flat, vec, vec, taps),
        check_vma=False,
    )
```

time: 1500 us -> 402 us (0.27)
  waiting for transfers between devices: 1250 us -> 194 us
  blocking collectives: 124 us -> 0 us
  starting transfers between devices: 4.37 us -> 97.1 us
  matrix products: 83.6 us -> 0 us
  Pallas kernels: 0 us -> 48.9 us
  local copies, waits for them, and re-layouts: 10.6 us -> 29.1 us
  other arithmetic: 7.46 us -> 22.8 us
    reduce_scatter x5 -> x0, waiting for transfers between devices: 939 us -> none  [the longest x1 213 us: shards(): lax.psum_scatter(d_down, ('dp', 'seq'), scatter_dimension=0, tiled=True)]
    all_gather x5 -> x0, waiting for transfers between devices: 270 us -> none  [the longest x1 81.2 us: shards(): lax.all_gather(w_gate, ('dp', 'seq'), axis=0, tiled=True)]
    ppermute x2 -> x70, waiting for transfers between devices: 2.14 us -> 187 us  [the longest x24 141 us: to_chip(): lax.ppermute(block, 'seq', [(i, i ^ 2 * k) for i in range(lax.axis_size('...]
    dot_general x15 -> x0, matrix products: 83.6 us -> none  [the longest x5 33.8 us: tdot(): lax.dot_general(left, right, (((0,), (0,)), ((), ())), preferred_element_...]
    unnamed x2 -> x0, blocking collectives: 83.1 us -> none
    ppermute x2 -> x70, starting transfers between devices: 3.93 us -> 68.1 us  [the longest x24 34 us: to_chip(): lax.ppermute(block, 'seq', [(i, i ^ 2 * k) for i in range(lax.axis_size('...]
    pallas_call x0 -> x6, Pallas kernels: none -> 48.9 us  [call(): pl.pallas_call(kernel, out_shape=out_shape, in_specs=[SMEM] * len(smem) +...]
    all_gather x1 -> x0, blocking collectives: 41.2 us -> none  [shards(): lax.all_gather(conv_taps, ('dp', 'seq'), axis=1, tiled=True)]
  transfers between devices with their start and end apart: 13 -> 74, of which waited for: 12 -> 33; matrix products, arithmetic and copies ran while one was open for 5% -> 9% of each run, Pallas kernels for 0% -> 7%
where the time goes in v1:
time: 402 us; the launch traced here: 394 us
  waiting for transfers between devices  194 us (48%)
  starting transfers between devices  97.1 us (24%)
  Pallas kernels  48.9 us (12%)
  local copies, waits for them, and re-layouts  29.1 us (7%)
  other arithmetic  22.8 us (6%)
    ppermute x24, waiting for transfers between devices, to_chip(): lax.ppermute(block, 'seq', [(i, i ^ 2 * k) for i in range(lax.axis_size('...  141 us
    pallas_call x6, Pallas kernels, call(): pl.pallas_call(kernel, out_shape=out_shape, in_specs=[SMEM] * len(smem) +...  48.9 us
    ppermute x24, waiting for transfers between devices, to_row(): lax.ppermute(block, 'dp', [(i, i ^ k) for i in range(lax.axis_size('dp'))])  40.3 us
    ppermute x24, starting transfers between devices, to_chip(): lax.ppermute(block, 'seq', [(i, i ^ 2 * k) for i in range(lax.axis_size('...  34 us
    ppermute x24, starting transfers between devices, to_row(): lax.ppermute(block, 'dp', [(i, i ^ k) for i in range(lax.axis_size('dp'))])  30.4 us
    all_to_all x4, starting transfers between devices, exchange(): return lax.all_to_all(pieces, 'seq', 0, 0, tiled=True)  29 us
    convert_element_type x6, local copies, waits for them, and re-layouts, rows_of(): return back.reshape(rows, columns * seq).astype(F32)  13.7 us
  transfers between devices with their start and end apart: 74, of which 33 were waited for; matrix products, arithmetic and copies ran while one was open for 9% of the time, Pallas kernels for 7%

profile of v1, /device:TPU:0, one launch (start us, length us, event | category | flops | bytes accessed | tf_op | source)
XLA Modules:
  0.0 394.2 jit_solution(7199411400812576973)
XLA Ops:
  0.6 5.1 %collective-permute-start.2 = (bf16[128,1024]{1,0:T(8,128)(2,1)}, bf16[128,1024]{1,0:T(8,128)(2,1)S(1)}, u32[]{:S(2)}, u32[]{:S(2)}) collective-permute-start(bf16[128,1024]{1,0:T(8,128)(2,1)} %bitcast.48), channel_id=1, source_target_pairs={{0,6},{1,7},{2,4},{3,5},{4,2},{5,3},{6,0},{7,1},{8,14},{9,15},{10,... | collective-permute-start | bytes 786440 | tf_op jit(solution)/shard_map/ppermute | solution.py:48
  10.4 5.0 %all-to-all-start = ((bf16[8,32,512]{2,1,0:T(8,128)(2,1)}), bf16[8,32,512]{2,1,0:T(8,128)(2,1)S(1)}, u32[]{:S(2)}, u32[]{:S(2)}) async-start(bf16[8,32,512]{2,1,0:T(8,128)(2,1)} %pad_maximum_fusion.1), calls=%async_computation | async-start | bytes 524288 | tf_op jit(solution)/shard_map/all_to_all | solution.py:101
  19.5 12.6 %collective-permute-done.1.refs_4_ = bf16[128,1024]{1,0:T(8,128)(2,1)S(1)} collective-permute-done((bf16[128,1024]{1,0:T(8,128)(2,1)}, bf16[128,1024]{1,0:T(8,128)(2,1)S(1)}, u32[]{:S(2)}, u32[]{:S(2)}) %collective-permute-start.1) | collective-permute-done | bytes 262176 | tf_op jit(solution)/shard_map/ppermute | solution.py:48
  44.7 5.6 %collective-permute-done.9.refs_11_ = bf16[256,512]{1,0:T(8,128)(2,1)S(1)} collective-permute-done((bf16[256,512]{1,0:T(8,128)(2,1)S(1)}, bf16[256,512]{1,0:T(8,128)(2,1)S(1)}, u32[]{:S(2)}, u32[]{:S(2)}) %collective-permute-start.9) | collective-permute-done | bytes 262176 | tf_op jit(solution)/shard_map/ppermute | solution.py:56
  50.2 4.7 %collective-permute-done.8.refs_10_ = bf16[256,512]{1,0:T(8,128)(2,1)S(1)} collective-permute-done((bf16[256,512]{1,0:T(8,128)(2,1)S(1)}, bf16[256,512]{1,0:T(8,128)(2,1)S(1)}, u32[]{:S(2)}, u32[]{:S(2)}) %collective-permute-start.8) | collective-permute-done | bytes 262176 | tf_op jit(solution)/shard_map/ppermute | solution.py:56
  56.4 6.7 %shard_map.177 = (bf16[1024,1024]{1,0:T(8,128)(2,1)}, bf16[1024,512]{1,0:T(8,128)(2,1)}, bf16[128,1152]{1,0:T(8,128)(2,1)}, f32[1024,384]{1,0:T(8,128)}, bf16[10...) custom-call(s32[8]{0:T(128)} %fusion.12.where, ...), custom_call_target="tpu_custom_call" | custom-call | tf_op jit(solution)/shard_map/pallas_call | solution.py:113
  67.6 15.6 %all-to-all-start.1 = ((bf16[8,32,1152]{2,1,0:T(8,128)(2,1)}), bf16[8,32,1152]{2,1,0:T(8,128)(2,1)S(1)}, u32[]{:S(2)}, u32[]{:S(2)}) async-start(bf16[8,32,1152]{2,1,0:T(8,128)(2,1)} %reshape.94), calls=%async_computation.1 | async-start | bytes 1179648 | tf_op jit(solution)/shard_map/all_to_all | solution.py:101
  93.7 9.9 %collective-permute-done.14 = bf16[128,1024]{1,0:T(8,128)(2,1)S(1)} collective-permute-done((bf16[128,1024]{1,0:T(8,128)(2,1)S(1)}, bf16[128,1024]{1,0:T(8,128)(2,1)S(1)}, u32[]{:S(2)}, u32[]{:S(2)}) %collective-permute-start.14) | collective-permute-done | bytes 262176 | tf_op jit(solution)/shard_map/ppermute | solution.py:48
  104.9 4.8 %collective-permute-done.16 = bf16[128,1024]{1,0:T(8,128)(2,1)S(1)} collective-permute-done((bf16[128,1024]{1,0:T(8,128)(2,1)S(1)}, bf16[128,1024]{1,0:T(8,128)(2,1)S(1)}, u32[]{:S(2)}, u32[]{:S(2)}) %collective-permute-start.16) | collective-permute-done | bytes 262176 | tf_op jit(solution)/shard_map/ppermute | solution.py:48
  109.7 13.6 %collective-permute-done.15 = bf16[128,1024]{1,0:T(8,128)(2,1)S(1)} collective-permute-done((bf16[128,1024]{1,0:T(8,128)(2,1)S(1)}, bf16[128,1024]{1,0:T(8,128)(2,1)S(1)}, u32[]{:S(2)}, u32[]{:S(2)}) %collective-permute-start.15) | collective-permute-done | bytes 262176 | tf_op jit(solution)/shard_map/ppermute | solution.py:48
  129.0 3.2 collective-permute-start.17
  133.4 3.4 collective-permute-done.19.refs_4_.refs_6_
  138.2 9.9 %collective-permute-done.18.refs_2_.refs_4_ = bf16[128,1024]{1,0:T(8,128)(2,1)S(1)} collective-permute-done((bf16[128,1024]{1,0:T(8,128)(2,1)}, bf16[128,1024]{1,0:T(8,128)(2,1)S(1)}, u32[]{:S(2)}, u32[]{:S(2)}) %collective-permute-start.18) | collective-permute-done | bytes 262176 | tf_op jit(solution)/shard_map/ppermute | solution.py:48
  150.7 4.7 %collective-permute-done.26.refs_6_.refs_14_ = bf16[256,1152]{1,0:T(8,128)(2,1)S(1)} collective-permute-done((bf16[256,1152]{1,0:T(8,128)(2,1)S(1)}, bf16[256,1152]{1,0:T(8,128)(2,1)S(1)}, u32[]{:S(2)}, u32[]{:S(2)}) %collective-permute-start.26) | collective-permute-done | bytes 589856 | tf_op jit(solution)/shard_map/ppermute | solution.py:56
  156.9 14.2 %shard_map.179 = (f32[384,1024]{1,0:T(8,128)}, bf16[384,1024]{1,0:T(8,128)(2,1)}, f32[384,1024]{1,0:T(8,128)}, bf16[384,1024]{1,0:T(8,128)(2,1)}, bf16[768,576]{1,0:T(8,128)(2,1)}, /*index=5*/bf16[768,1152]{1,0:T(8,128)(2,1)}) custom-call(s32[4]{0:T(128)} %iota_xor_fusion.dwhere, bf16[128,1024]{1,0:T(8,128)(2,1)} %copy-done.30, ...), custom_call_target="tpu_custom_call" | custom-call | tf_op jit(solution)/shard_map/pallas_call | solution.py:113
  175.5 6.2 %shard_map.178 = (f32[128,1024]{1,0:T(8,128)}, bf16[128,1024]{1,0:T(8,128)(2,1)}, f32[128,1024]{1,0:T(8,128)}, bf16[128,1024]{1,0:T(8,128)(2,1)}, bf16[256,576]{1,0:T(8,128)(2,1)}, /*index=5*/bf16[256,1152]{1,0:T(8,128)(2,1)}) custom-call(s32[4]{0:T(128)} %iota_xor_fusion.dwhere, bf16[128,1024]{1,0:T(8,128)(2,1)} %multiply_convert_fusion.refs_0_, ...), custom_call_target="tpu_custom_call" | custom-call | tf_op jit(solution)/shard_map/pallas_call | solution.py:113
  183.9 3.6 collective-permute-start.46
  187.6 4.4 %collective-permute-done.44 = bf16[128,1024]{1,0:T(8,128)(2,1)S(1)} collective-permute-done((bf16[128,1024]{1,0:T(8,128)(2,1)S(1)}, bf16[128,1024]{1,0:T(8,128)(2,1)S(1)}, u32[]{:S(2)}, u32[]{:S(2)}) %collective-permute-start.44) | collective-permute-done | bytes 262176 | tf_op jit(solution)/shard_map/ppermute | solution.py:48
  192.0 8.5 %collective-permute-done.46 = bf16[128,1024]{1,0:T(8,128)(2,1)S(1)} collective-permute-done((bf16[128,1024]{1,0:T(8,128)(2,1)S(1)}, bf16[128,1024]{1,0:T(8,128)(2,1)S(1)}, u32[]{:S(2)}, u32[]{:S(2)}) %collective-permute-start.46) | collective-permute-done | bytes 262176 | tf_op jit(solution)/shard_map/ppermute | solution.py:48
  200.4 9.6 %collective-permute-done.45 = bf16[128,1024]{1,0:T(8,128)(2,1)S(1)} collective-permute-done((bf16[128,1024]{1,0:T(8,128)(2,1)S(1)}, bf16[128,1024]{1,0:T(8,128)(2,1)S(1)}, u32[]{:S(2)}, u32[]{:S(2)}) %collective-permute-start.45) | collective-permute-done | bytes 262176 | tf_op jit(solution)/shard_map/ppermute | solution.py:48
  215.6 6.7 %collective-permute-done.49.refs_6_ = bf16[128,1024]{1,0:T(8,128)(2,1)S(1)} collective-permute-done((bf16[128,1024]{1,0:T(8,128)(2,1)S(1)}, bf16[128,1024]{1,0:T(8,128)(2,1)S(1)}, u32[]{:S(2)}, u32[]{:S(2)}) %collective-permute-start.49) | collective-permute-done | bytes 262176 | tf_op jit(solution)/shard_map/ppermute | solution.py:48
  222.3 12.4 %collective-permute-done.48.refs_4_ = bf16[128,1024]{1,0:T(8,128)(2,1)S(1)} collective-permute-done((bf16[128,1024]{1,0:T(8,128)(2,1)S(1)}, bf16[128,1024]{1,0:T(8,128)(2,1)S(1)}, u32[]{:S(2)}, u32[]{:S(2)}) %collective-permute-start.48) | collective-permute-done | bytes 262176 | tf_op jit(solution)/shard_map/ppermute | solution.py:48
  238.2 7.5 %shard_map.180 = (f32[128,1024]{1,0:T(8,128)}, f32[128,1024]{1,0:T(8,128)}, f32[128,1024]{1,0:T(8,128)}, f32[128,1024]{1,0:T(8,128)}, bf16[512,1024]{1,0:T(8,128...) custom-call(s32[8]{0:T(128)} %fusion.12.where, ...), custom_call_target="tpu_custom_call" | custom-call | tf_op jit(solution)/shard_map/pallas_call | solution.py:113
  245.7 5.0 %shard_map.181 = (f32[32,1152]{1,0:T(8,128)}, bf16[32,1152]{1,0:T(8,128)(2,1)}, bf16[32,1152]{1,0:T(8,128)(2,1)}, bf16[32,1152]{1,0:T(8,128)(2,1)}, f32[256,384]...) custom-call(s32[4]{0:T(128)} %iota_xor_fusion.dwhere, ...), custom_call_target="tpu_custom_call" | custom-call | tf_op jit(solution)/shard_map/pallas_call | solution.py:113
  253.0 9.3 %shard_map.182 = (f32[256,1152]{1,0:T(8,128)}, bf16[256,1152]{1,0:T(8,128)(2,1)}, bf16[256,1152]{1,0:T(8,128)(2,1)}, bf16[256,1152]{1,0:T(8,128)(2,1)}, f32[144,...) custom-call(s32[4]{0:T(128)} %iota_xor_fusion.dwhere, ...), custom_call_target="tpu_custom_call" | custom-call | tf_op jit(solution)/shard_map/pallas_call | solution.py:113
  279.1 4.0 %all-to-all-start.2 = ((bf16[8,32,384]{2,1,0:T(8,128)(2,1)}), bf16[8,32,384]{2,1,0:T(8,128)(2,1)}, u32[]{:S(2)}, u32[]{:S(2)}) async-start(bf16[8,32,384]{2,1,0:T(8,128)(2,1)} %bitcast.13), calls=%async_computation.2 | async-start | bytes 393216 | tf_op jit(solution)/shard_map/all_to_all | solution.py:101
  284.5 6.9 %all-to-all-done.2 = bf16[8,32,384]{2,1,0:T(8,128)(2,1)} async-done(((bf16[8,32,384]{2,1,0:T(8,128)(2,1)}), bf16[8,32,384]{2,1,0:T(8,128)(2,1)}, u32[]{:S(2)}, u32[]{:S(2)}) %all-to-all-start.2) | async-done | bytes 196640 | tf_op jit(solution)/shard_map/all_to_all | solution.py:101
  302.8 17.3 %collective-permute-done.68 = bf16[144,1024]{1,0:T(8,128)(2,1)S(1)} collective-permute-done((bf16[144,1024]{1,0:T(8,128)(2,1)}, bf16[144,1024]{1,0:T(8,128)(2,1)S(1)}, u32[]{:S(2)}, u32[]{:S(2)}) %collective-permute-start.68) | collective-permute-done | bytes 294944 | tf_op jit(solution)/shard_map/ppermute | solution.py:56
  326.9 4.3 %all-to-all-start.3 = ((bf16[8,32,1152]{2,1,0:T(8,128)(2,1)}), bf16[8,32,1152]{2,1,0:T(8,128)(2,1)}, u32[]{:S(2)}, u32[]{:S(2)}) async-start(bf16[8,32,1152]{2,1,0:T(8,128)(2,1)} %bitcast.15), calls=%async_computation.3 | async-start | bytes 1179648 | tf_op jit(solution)/shard_map/all_to_all | solution.py:101
  333.4 12.0 %collective-permute-done.55 = bf16[128,1024]{1,0:T(8,128)(2,1)S(1)} collective-permute-done((bf16[128,1024]{1,0:T(8,128)(2,1)}, bf16[128,1024]{1,0:T(8,128)(2,1)S(1)}, u32[]{:S(2)}, u32[]{:S(2)}) %collective-permute-start.55) | collective-permute-done | bytes 262176 | tf_op jit(solution)/shard_map/ppermute | solution.py:48
  352.4 9.0 %collective-permute-done.41 = bf16[128,1024]{1,0:T(8,128)(2,1)S(1)} collective-permute-done((bf16[128,1024]{1,0:T(8,128)(2,1)S(1)}, bf16[128,1024]{1,0:T(8,128)(2,1)S(1)}, u32[]{:S(2)}, u32[]{:S(2)}) %collective-permute-start.41) | collective-permute-done | bytes 262176 | tf_op jit(solution)/shard_map/ppermute | solution.py:48
  361.4 21.6 %collective-permute-done.40 = bf16[128,1024]{1,0:T(8,128)(2,1)S(1)} collective-permute-done((bf16[128,1024]{1,0:T(8,128)(2,1)S(1)}, bf16[128,1024]{1,0:T(8,128)(2,1)S(1)}, u32[]{:S(2)}, u32[]{:S(2)}) %collective-permute-start.40) | collective-permute-done | bytes 262176 | tf_op jit(solution)/shard_map/ppermute | solution.py:48
  (323 shorter events, 125.1 us)
Async XLA Ops:
  5.8 26.3 %collective-permute-start.1 = (bf16[128,1024]{1,0:T(8,128)(2,1)}, bf16[128,1024]{1,0:T(8,128)(2,1)S(1)}, u32[]{:S(2)}, u32[]{:S(2)}) collective-permute-start(bf16[128,1024]{1,0:T(8,128)(2,1)} %bitcast.49), channel_id=1, source_target_pairs={{0,4},{1,5},{2,6},{3,7},{4,0},{5,1},{6,2},{7,3},{8,12},{9,13},{10,... | collective-permute-start | bytes 786440 | tf_op jit(solution)/shard_map/ppermute | solution.py:48
  5.8 26.3 %collective-permute-start = (bf16[128,1024]{1,0:T(8,128)(2,1)}, bf16[128,1024]{1,0:T(8,128)(2,1)S(1)}, u32[]{:S(2)}, u32[]{:S(2)}) collective-permute-start(bf16[128,1024]{1,0:T(8,128)(2,1)} %bitcast.50), channel_id=1, source_target_pairs={{0,2},{1,3},{2,0},{3,1},{4,6},{5,7},{6,4},{7,5},{8,10},{9,11},{10,... | collective-permute-start | bytes 786440 | tf_op jit(solution)/shard_map/ppermute | solution.py:48
  10.4 29.7 %all-to-all-start = ((bf16[8,32,512]{2,1,0:T(8,128)(2,1)}), bf16[8,32,512]{2,1,0:T(8,128)(2,1)S(1)}, u32[]{:S(2)}, u32[]{:S(2)}) async-start(bf16[8,32,512]{2,1,0:T(8,128)(2,1)} %pad_maximum_fusion.1), calls=%async_computation | async-start | bytes 524288 | tf_op jit(solution)/shard_map/all_to_all | solution.py:101
  63.2 26.6 %collective-permute-start.23 = (bf16[128,1024]{1,0:T(8,128)(2,1)S(1)}, bf16[128,1024]{1,0:T(8,128)(2,1)S(1)}, u32[]{:S(2)}, u32[]{:S(2)}) collective-permute-start(bf16[128,1024]{1,0:T(8,128)(2,1)S(1)} %bitcast.56), channel_id=1, source_target_pairs={{0,6},{1,7},{2,4},{3,5},{4,2},{5,3},{6,0},{7,1},{8,14},{9,15},{10,... | collective-permute-start | bytes 786440 | tf_op jit(solution)/shard_map/ppermute | solution.py:48
  65.9 24.0 %collective-permute-start.22 = (bf16[128,1024]{1,0:T(8,128)(2,1)S(1)}, bf16[128,1024]{1,0:T(8,128)(2,1)S(1)}, u32[]{:S(2)}, u32[]{:S(2)}) collective-permute-start(bf16[128,1024]{1,0:T(8,128)(2,1)S(1)} %bitcast.57), channel_id=1, source_target_pairs={{0,4},{1,5},{2,6},{3,7},{4,0},{5,1},{6,2},{7,3},{8,12},{9,13},{10,... | collective-permute-start | bytes 786440 | tf_op jit(solution)/shard_map/ppermute | solution.py:48
  65.9 25.7 %collective-permute-start.21 = (bf16[128,1024]{1,0:T(8,128)(2,1)S(1)}, bf16[128,1024]{1,0:T(8,128)(2,1)S(1)}, u32[]{:S(2)}, u32[]{:S(2)}) collective-permute-start(bf16[128,1024]{1,0:T(8,128)(2,1)S(1)} %bitcast.58), channel_id=1, source_target_pairs={{0,2},{1,3},{2,0},{3,1},{4,6},{5,7},{6,4},{7,5},{8,10},{9,11},{10,... | collective-permute-start | bytes 786440 | tf_op jit(solution)/shard_map/ppermute | solution.py:48
  67.6 59.0 %all-to-all-start.1 = ((bf16[8,32,1152]{2,1,0:T(8,128)(2,1)}), bf16[8,32,1152]{2,1,0:T(8,128)(2,1)S(1)}, u32[]{:S(2)}, u32[]{:S(2)}) async-start(bf16[8,32,1152]{2,1,0:T(8,128)(2,1)} %reshape.94), calls=%async_computation.1 | async-start | bytes 1179648 | tf_op jit(solution)/shard_map/all_to_all | solution.py:101
  87.4 22.3 %collective-permute-start.16 = (bf16[128,1024]{1,0:T(8,128)(2,1)S(1)}, bf16[128,1024]{1,0:T(8,128)(2,1)S(1)}, u32[]{:S(2)}, u32[]{:S(2)}) collective-permute-start(bf16[128,1024]{1,0:T(8,128)(2,1)S(1)} %get-tuple-element.214), channel_id=1, source_target_pairs={{0,6},{1,7},{2,4},{3,5},{4,2},{5,3},{6,0},{7,1},{8,14},{9,15},{10,... | collective-permute-start | bytes 786440 | tf_op jit(solution)/shard_map/ppermute | solution.py:48
  89.8 33.5 %collective-permute-start.15 = (bf16[128,1024]{1,0:T(8,128)(2,1)S(1)}, bf16[128,1024]{1,0:T(8,128)(2,1)S(1)}, u32[]{:S(2)}, u32[]{:S(2)}) collective-permute-start(bf16[128,1024]{1,0:T(8,128)(2,1)S(1)} %get-tuple-element.215), channel_id=1, source_target_pairs={{0,4},{1,5},{2,6},{3,7},{4,0},{5,1},{6,2},{7,3},{8,12},{9,13},{10,... | collective-permute-start | bytes 786440 | tf_op jit(solution)/shard_map/ppermute | solution.py:48
  89.9 36.7 %collective-permute-start.30 = (bf16[144,1024]{1,0:T(8,128)(2,1)S(1)}, bf16[144,1024]{1,0:T(8,128)(2,1)S(1)}, u32[]{:S(2)}, u32[]{:S(2)}) collective-permute-start(bf16[144,1024]{1,0:T(8,128)(2,1)S(1)} %copy-done.13), channel_id=1, source_target_pairs={{0,24},{8,16},{16,8},{24,0},{1,25},{9,17},{17,9},{25,1},{2,26},{10... | collective-permute-start | bytes 884744 | tf_op jit(solution)/shard_map/ppermute | solution.py:56
  91.6 37.4 %collective-permute-start.29 = (bf16[144,1024]{1,0:T(8,128)(2,1)S(1)}, bf16[144,1024]{1,0:T(8,128)(2,1)S(1)}, u32[]{:S(2)}, u32[]{:S(2)}) collective-permute-start(bf16[144,1024]{1,0:T(8,128)(2,1)S(1)} %copy-done.13), channel_id=1, source_target_pairs={{0,16},{8,24},{16,0},{24,8},{1,17},{9,25},{17,1},{25,9},{2,18},{10... | collective-permute-start | bytes 884744 | tf_op jit(solution)/shard_map/ppermute | solution.py:56
  103.5 25.5 %collective-permute-start.28 = (bf16[144,1024]{1,0:T(8,128)(2,1)S(1)}, bf16[144,1024]{1,0:T(8,128)(2,1)S(1)}, u32[]{:S(2)}, u32[]{:S(2)}) collective-permute-start(bf16[144,1024]{1,0:T(8,128)(2,1)S(1)} %copy-done.13), channel_id=1, source_target_pairs={{0,8},{8,0},{16,24},{24,16},{1,9},{9,1},{17,25},{25,17},{2,10},{10... | collective-permute-start | bytes 884744 | tf_op jit(solution)/shard_map/ppermute | solution.py:56
  109.7 22.5 %collective-permute-start.35 = (bf16[128,1024]{1,0:T(8,128)(2,1)S(1)}, bf16[128,1024]{1,0:T(8,128)(2,1)}, u32[]{:S(2)}, u32[]{:S(2)}) collective-permute-start(bf16[128,1024]{1,0:T(8,128)(2,1)S(1)} %collective-permute-done.21.refs_6_.refs_10_), channel_id=1, source_target_pairs={{0,1},{1,0},{2,3},{3,2},{4,5},{5,4},{6,7},{7,6},{8,9},{9,8},{10,11... | collective-permute-start | bytes 786440 | tf_op jit(solution)/shard_map/ppermute | solution.py:52
  127.3 23.0 %collective-permute-start.27 = (bf16[256,1152]{1,0:T(8,128)(2,1)S(1)}, bf16[256,1152]{1,0:T(8,128)(2,1)S(1)}, u32[]{:S(2)}, u32[]{:S(2)}) collective-permute-start(bf16[256,1152]{1,0:T(8,128)(2,1)S(1)} %bitcast.43), channel_id=1, source_target_pairs={{0,24},{8,16},{16,8},{24,0},{1,25},{9,17},{17,9},{25,1},{2,26},{10... | collective-permute-start | bytes 1769480 | tf_op jit(solution)/shard_map/ppermute | solution.py:56
  132.2 23.2 %collective-permute-start.26 = (bf16[256,1152]{1,0:T(8,128)(2,1)S(1)}, bf16[256,1152]{1,0:T(8,128)(2,1)S(1)}, u32[]{:S(2)}, u32[]{:S(2)}) collective-permute-start(bf16[256,1152]{1,0:T(8,128)(2,1)S(1)} %bitcast.44), channel_id=1, source_target_pairs={{0,16},{8,24},{16,0},{24,8},{1,17},{9,25},{17,1},{25,9},{2,18},{10... | collective-permute-start | bytes 1769480 | tf_op jit(solution)/shard_map/ppermute | solution.py:56
  187.6 22.4 %collective-permute-start.45 = (bf16[128,1024]{1,0:T(8,128)(2,1)S(1)}, bf16[128,1024]{1,0:T(8,128)(2,1)S(1)}, u32[]{:S(2)}, u32[]{:S(2)}) collective-permute-start(bf16[128,1024]{1,0:T(8,128)(2,1)S(1)} %get-tuple-element.204), channel_id=1, source_target_pairs={{0,4},{1,5},{2,6},{3,7},{4,0},{5,1},{6,2},{7,3},{8,12},{9,13},{10,... | collective-permute-start | bytes 786440 | tf_op jit(solution)/shard_map/ppermute | solution.py:48
  187.6 77.4 %collective-permute-start.38 = (bf16[384,1024]{1,0:T(8,128)(2,1)}, bf16[384,1024]{1,0:T(8,128)(2,1)}, u32[]{:S(2)}, u32[]{:S(2)}) collective-permute-start(bf16[384,1024]{1,0:T(8,128)(2,1)} %get-tuple-element.107), channel_id=1, source_target_pairs={{0,1},{1,0},{2,3},{3,2},{4,5},{5,4},{6,7},{7,6},{8,9},{9,8},{10,11... | collective-permute-start | bytes 2359304 | tf_op jit(solution)/shard_map/ppermute | solution.py:52
  213.8 20.9 %collective-permute-start.47 = (bf16[128,1024]{1,0:T(8,128)(2,1)S(1)}, bf16[128,1024]{1,0:T(8,128)(2,1)S(1)}, u32[]{:S(2)}, u32[]{:S(2)}) collective-permute-start(bf16[128,1024]{1,0:T(8,128)(2,1)S(1)} %fusion.15.refs_0_), channel_id=1, source_target_pairs={{0,2},{1,3},{2,0},{3,1},{4,6},{5,7},{6,4},{7,5},{8,10},{9,11},{10,... | collective-permute-start | bytes 786440 | tf_op jit(solution)/shard_map/ppermute | solution.py:48
  267.1 31.8 %collective-permute-start.54 = (bf16[512,1024]{1,0:T(8,128)(2,1)}, bf16[512,1024]{1,0:T(8,128)(2,1)}, u32[]{:S(2)}, u32[]{:S(2)}) collective-permute-start(bf16[512,1024]{1,0:T(8,128)(2,1)} %get-tuple-element.121), channel_id=1, source_target_pairs={{0,1},{1,0},{2,3},{3,2},{4,5},{5,4},{6,7},{7,6},{8,9},{9,8},{10,11... | collective-permute-start | bytes 3145736 | tf_op jit(solution)/shard_map/ppermute | solution.py:52
  269.3 28.2 %collective-permute-start.67 = (bf16[144,1024]{1,0:T(8,128)(2,1)}, bf16[144,1024]{1,0:T(8,128)(2,1)}, u32[]{:S(2)}, u32[]{:S(2)}) collective-permute-start(bf16[144,1024]{1,0:T(8,128)(2,1)} %get-tuple-element.156), channel_id=1, source_target_pairs={{0,8},{8,0},{16,24},{24,16},{1,9},{9,1},{17,25},{25,17},{2,10},{10... | collective-permute-start | bytes 884744 | tf_op jit(solution)/shard_map/ppermute | solution.py:56
  272.6 48.2 %collective-permute-start.64 = (bf16[256,1152]{1,0:T(8,128)(2,1)}, bf16[256,1152]{1,0:T(8,128)(2,1)}, u32[]{:S(2)}, u32[]{:S(2)}) collective-permute-start(bf16[256,1152]{1,0:T(8,128)(2,1)} %get-tuple-element.149), channel_id=1, source_target_pairs={{0,8},{8,0},{16,24},{24,16},{1,9},{9,1},{17,25},{25,17},{2,10},{10... | collective-permute-start | bytes 1769480 | tf_op jit(solution)/shard_map/ppermute | solution.py:56
  273.2 49.6 %collective-permute-start.65 = (bf16[256,1152]{1,0:T(8,128)(2,1)}, bf16[256,1152]{1,0:T(8,128)(2,1)}, u32[]{:S(2)}, u32[]{:S(2)}) collective-permute-start(bf16[256,1152]{1,0:T(8,128)(2,1)} %get-tuple-element.150), channel_id=1, source_target_pairs={{0,16},{8,24},{16,0},{24,8},{1,17},{9,25},{17,1},{25,9},{2,18},{10... | collective-permute-start | bytes 1769480 | tf_op jit(solution)/shard_map/ppermute | solution.py:56
  277.0 47.1 %collective-permute-start.66 = (bf16[256,1152]{1,0:T(8,128)(2,1)}, bf16[256,1152]{1,0:T(8,128)(2,1)}, u32[]{:S(2)}, u32[]{:S(2)}) collective-permute-start(bf16[256,1152]{1,0:T(8,128)(2,1)} %get-tuple-element.151), channel_id=1, source_target_pairs={{0,24},{8,16},{16,8},{24,0},{1,25},{9,17},{17,9},{25,1},{2,26},{10... | collective-permute-start | bytes 1769480 | tf_op jit(solution)/shard_map/ppermute | solution.py:56
  297.5 22.5 %collective-permute-start.68 = (bf16[144,1024]{1,0:T(8,128)(2,1)}, bf16[144,1024]{1,0:T(8,128)(2,1)S(1)}, u32[]{:S(2)}, u32[]{:S(2)}) collective-permute-start(bf16[144,1024]{1,0:T(8,128)(2,1)} %get-tuple-element.157), channel_id=1, source_target_pairs={{0,16},{8,24},{16,0},{24,8},{1,17},{9,25},{17,1},{25,9},{2,18},{10... | collective-permute-start | bytes 884744 | tf_op jit(solution)/shard_map/ppermute | solution.py:56
  298.9 21.8 %collective-permute-start.69 = (bf16[144,1024]{1,0:T(8,128)(2,1)}, bf16[144,1024]{1,0:T(8,128)(2,1)}, u32[]{:S(2)}, u32[]{:S(2)}) collective-permute-start(bf16[144,1024]{1,0:T(8,128)(2,1)} %get-tuple-element.158), channel_id=1, source_target_pairs={{0,24},{8,16},{16,8},{24,0},{1,25},{9,17},{17,9},{25,1},{2,26},{10... | collective-permute-start | bytes 884744 | tf_op jit(solution)/shard_map/ppermute | solution.py:56
  320.8 31.7 %collective-permute-start.31 = (bf16[128,1024]{1,0:T(8,128)(2,1)}, bf16[128,1024]{1,0:T(8,128)(2,1)S(1)}, u32[]{:S(2)}, u32[]{:S(2)}) collective-permute-start(bf16[128,1024]{1,0:T(8,128)(2,1)} %get-tuple-element.99), channel_id=1, source_target_pairs={{0,1},{1,0},{2,3},{3,2},{4,5},{5,4},{6,7},{7,6},{8,9},{9,8},{10,11... | collective-permute-start | bytes 786440 | tf_op jit(solution)/shard_map/ppermute | solution.py:52
  320.8 31.7 %collective-permute-start.39 = (bf16[128,1024]{1,0:T(8,128)(2,1)}, bf16[128,1024]{1,0:T(8,128)(2,1)S(1)}, u32[]{:S(2)}, u32[]{:S(2)}) collective-permute-start(bf16[128,1024]{1,0:T(8,128)(2,1)} %get-tuple-element.205), channel_id=1, source_target_pairs={{0,2},{1,3},{2,0},{3,1},{4,6},{5,7},{6,4},{7,5},{8,10},{9,11},{10,... | collective-permute-start | bytes 786440 | tf_op jit(solution)/shard_map/ppermute | solution.py:48
  320.8 24.6 %collective-permute-start.55 = (bf16[128,1024]{1,0:T(8,128)(2,1)}, bf16[128,1024]{1,0:T(8,128)(2,1)S(1)}, u32[]{:S(2)}, u32[]{:S(2)}) collective-permute-start(bf16[128,1024]{1,0:T(8,128)(2,1)} %get-tuple-element.210), channel_id=1, source_target_pairs={{0,2},{1,3},{2,0},{3,1},{4,6},{5,7},{6,4},{7,5},{8,10},{9,11},{10,... | collective-permute-start | bytes 786440 | tf_op jit(solution)/shard_map/ppermute | solution.py:48
  322.8 25.1 %collective-permute-start.57 = (bf16[128,1024]{1,0:T(8,128)(2,1)}, bf16[128,1024]{1,0:T(8,128)(2,1)S(1)}, u32[]{:S(2)}, u32[]{:S(2)}) collective-permute-start(bf16[128,1024]{1,0:T(8,128)(2,1)} %get-tuple-element.211), channel_id=1, source_target_pairs={{0,6},{1,7},{2,4},{3,5},{4,2},{5,3},{6,0},{7,1},{8,14},{9,15},{10,... | collective-permute-start | bytes 786440 | tf_op jit(solution)/shard_map/ppermute | solution.py:48
  324.1 27.0 %collective-permute-start.56 = (bf16[128,1024]{1,0:T(8,128)(2,1)}, bf16[128,1024]{1,0:T(8,128)(2,1)S(1)}, u32[]{:S(2)}, u32[]{:S(2)}) collective-permute-start(bf16[128,1024]{1,0:T(8,128)(2,1)} %get-tuple-element.212), channel_id=1, source_target_pairs={{0,4},{1,5},{2,6},{3,7},{4,0},{5,1},{6,2},{7,3},{8,12},{9,13},{10,... | collective-permute-start | bytes 786440 | tf_op jit(solution)/shard_map/ppermute | solution.py:48
  326.9 57.4 %all-to-all-start.3 = ((bf16[8,32,1152]{2,1,0:T(8,128)(2,1)}), bf16[8,32,1152]{2,1,0:T(8,128)(2,1)}, u32[]{:S(2)}, u32[]{:S(2)}) async-start(bf16[8,32,1152]{2,1,0:T(8,128)(2,1)} %bitcast.15), calls=%async_computation.3 | async-start | bytes 1179648 | tf_op jit(solution)/shard_map/all_to_all | solution.py:101
  347.9 35.1 %collective-permute-start.40 = (bf16[128,1024]{1,0:T(8,128)(2,1)S(1)}, bf16[128,1024]{1,0:T(8,128)(2,1)S(1)}, u32[]{:S(2)}, u32[]{:S(2)}) collective-permute-start(bf16[128,1024]{1,0:T(8,128)(2,1)S(1)} %copy-done.49), channel_id=1, source_target_pairs={{0,4},{1,5},{2,6},{3,7},{4,0},{5,1},{6,2},{7,3},{8,12},{9,13},{10,... | collective-permute-start | bytes 786440 | tf_op jit(solution)/shard_map/ppermute | solution.py:48
  (119 other events, 1299.3 us)
